TPU v7x, 32 devices: a whole 2x2x4 slice. The times are simulated.
32 devices in a mesh: dp: 2 (over core), blk: 4 (over y, x), head: 4 (over z).
Axes of the slice: x: 2, y: 2, z: 4, core: 2. Of those that a mesh axis runs over, the one named last changes fastest.
Arguments:
- activations: bfloat16 [2, 2, 2048, 1536], P(None, 'dp', ('blk', 'head')), may hold values from -6 to 6
- segments: int32 [2, 2, 2048], P(None, 'dp', 'blk'), may hold values from 0 to 15, never falling along the last dimension, each value on 1 to 1024 neighbouring positions
- cotangent: bfloat16 [2, 2, 2048, 1536], P(None, 'dp', ('blk', 'head')), may hold values from -6 to 6
- norm_gain_one: bfloat16 [1536], P(('dp', 'blk')), may hold values from 0.5 to 1.5
- query_weight: bfloat16 [1536, 1536], P(('dp', 'blk')), may hold values from -0.15625 to 0.15625
- key_weight: bfloat16 [1536, 768], P(('dp', 'blk')), may hold values from -0.15625 to 0.15625
- value_weight: bfloat16 [1536, 768], P(('dp', 'blk')), may hold values from -0.15625 to 0.15625
- output_weight: bfloat16 [1536, 1536], P(('dp', 'blk')), may hold values from -1.25 to 1.25
- norm_gain_two: bfloat16 [1536], P(('dp', 'blk')), may hold values from 0.5 to 1.5
- gate_weight: bfloat16 [1536, 4096], P(('dp', 'blk')), may hold values from -0.15625 to 0.15625
- up_weight: bfloat16 [1536, 4096], P(('dp', 'blk')), may hold values from -0.15625 to 0.15625
- down_weight: bfloat16 [4096, 1536], P(('dp', 'blk')), may hold values from -0.09375 to 0.09375
Outputs:
- block_out: bfloat16 [2, 2, 2048, 1536], P(None, 'dp', ('blk', 'head'))
- grad_input: bfloat16 [2, 2, 2048, 1536], P(None, 'dp', ('blk', 'head'))
- grad_gain_one: float32 [1536], P(('dp', 'blk'))
- grad_query: float32 [1536, 1536], P(('dp', 'blk'))
- grad_key: float32 [1536, 768], P(('dp', 'blk'))
- grad_value: float32 [1536, 768], P(('dp', 'blk'))
- grad_output: float32 [1536, 1536], P(('dp', 'blk'))
- grad_gain_two: float32 [1536], P(('dp', 'blk'))
- grad_gate: float32 [1536, 4096], P(('dp', 'blk'))
- grad_up: float32 [1536, 4096], P(('dp', 'blk'))
- grad_down: float32 [4096, 1536], P(('dp', 'blk'))
Inputs may be any that keep to these rules, and one draw needn't show every extreme that they name: `segments`: along each sequence the segment numbers never fall and every number is used; a document has at most 1024 tokens, and in every sequence one has exactly that many.
All inputs are finite; a program needn't handle non-finite values.
Results may differ from a plain program's by a relative error of at most 0.023.
Values may be sent and summed in bfloat16 or wider, within the bound.
No kernel may reach another device: no remote copies, remote signals or barrier semaphores. Data moves between devices by JAX's collectives and lax.ppermute only.
A program may use at most 320 MiB of HBM per device.

v0:
```python
import math
import jax
import jax.numpy as jnp
from jax import lax
from jax.sharding import PartitionSpec as P

D = 1536
QH = 16
KVH = 8
HD = 96
FF = 4096
EPS = 1e-05
NEG = -1e30


def shortened(value):
    return jax.tree.map(lambda a: a.astype(jnp.bfloat16) if a.dtype == jnp.float32 else a, value)


def plain_dot(left, right):
    return jnp.dot(left, right, preferred_element_type=jnp.float32)


def first_dot(left, right):
    return lax.dot_general(
        left, right, (((0,), (0,)), ((), ())), preferred_element_type=jnp.float32
    )


def last_dot(left, right):
    return lax.dot_general(
        left, right, (((1,), (1,)), ((), ())), preferred_element_type=jnp.float32
    )


def normalize(values):
    factor = lax.rsqrt(jnp.mean(values * values, -1, keepdims=True) + EPS)
    return (values * factor, factor)


def norm_back(grad_norm, gain, normed, factor):
    scaled = grad_norm * gain
    return factor * (scaled - normed * jnp.mean(scaled * normed, -1, keepdims=True))


def per_device(
    activations,
    segments,
    cotangent,
    norm_gain_one,
    query_weight,
    key_weight,
    value_weight,
    output_weight,
    norm_gain_two,
    gate_weight,
    up_weight,
    down_weight,
):
    shards = (
        norm_gain_one,
        query_weight,
        key_weight,
        value_weight,
        output_weight,
        norm_gain_two,
        gate_weight,
        up_weight,
        down_weight,
    )
    head_count = lax.axis_size("head")
    cycle_count = lax.axis_size("blk")
    tok_rows = activations.shape[2]
    span_len = tok_rows * head_count
    seq_len = span_len * cycle_count
    heads_here = QH // head_count
    kv_repeat = max(1, head_count // KVH)
    kv_here = KVH * kv_repeat // head_count
    group_size = heads_here // kv_here
    block_rows = span_len if span_len <= 1024 else 1024
    block_count = span_len // block_rows
    scale = 1.0 / math.sqrt(HD)
    first_pos = lax.axis_index("blk") * span_len
    full_shapes = (
        (D,),
        (D, QH * HD),
        (D, KVH * HD),
        (D, KVH * HD),
        (QH * HD, D),
        (D,),
        (D, FF),
        (D, FF),
        (FF, D),
    )
    totals = tuple((jnp.zeros(shape_full, jnp.float32) for shape_full in full_shapes))
    results = []
    grads_x = []
    for batch_index in range(activations.shape[0]):
        seg_rows = segments[batch_index, 0]
        cot_rows = cotangent[batch_index, 0]
        gain_one = lax.all_gather(shards[0], ("dp", "blk"), axis=0, tiled=True)
        query_w = lax.all_gather(shards[1], ("dp", "blk"), axis=0, tiled=True)
        key_w = lax.all_gather(shards[2], ("dp", "blk"), axis=0, tiled=True)
        value_w = lax.all_gather(shards[3], ("dp", "blk"), axis=0, tiled=True)
        out_w = lax.all_gather(shards[4], ("dp", "blk"), axis=0, tiled=True)
        gain_two = lax.all_gather(shards[5], ("dp", "blk"), axis=0, tiled=True)
        gate_w = lax.all_gather(shards[6], ("dp", "blk"), axis=0, tiled=True)
        up_w = lax.all_gather(shards[7], ("dp", "blk"), axis=0, tiled=True)
        down_w = lax.all_gather(shards[8], ("dp", "blk"), axis=0, tiled=True)
        gain_one_f = gain_one.astype(jnp.float32)
        gain_two_f = gain_two.astype(jnp.float32)
        x_float = activations[batch_index, 0].astype(jnp.float32)
        normed_one, factor_one = normalize(x_float)
        input_one = (normed_one * gain_one_f).astype(jnp.bfloat16)
        queries = plain_dot(input_one, query_w).astype(jnp.bfloat16).reshape(tok_rows, QH, HD)
        keys = plain_dot(input_one, key_w).astype(jnp.bfloat16).reshape(tok_rows, KVH, HD)
        values = plain_dot(input_one, value_w).astype(jnp.bfloat16).reshape(tok_rows, KVH, HD)
        if kv_repeat > 1:
            keys = jnp.repeat(keys, kv_repeat, axis=1)
            values = jnp.repeat(values, kv_repeat, axis=1)
        head_q = lax.all_to_all(queries, "head", split_axis=1, concat_axis=0, tiled=True)
        head_k = lax.all_to_all(keys, "head", split_axis=1, concat_axis=0, tiled=True)
        head_v = lax.all_to_all(values, "head", split_axis=1, concat_axis=0, tiled=True)
        query_blocks = head_q.reshape(block_count, block_rows, kv_here, group_size, HD)
        pos_blocks = (first_pos + jnp.arange(span_len, dtype=jnp.int32)).reshape(
            block_count, block_rows
        )
        seg_blocks = seg_rows.reshape(block_count, block_rows)
        key_piece = lax.all_gather(head_k, "blk", axis=0, tiled=True)
        value_piece = lax.all_gather(head_v, "blk", axis=0, tiled=True)
        seg_piece = lax.all_gather(seg_rows, "blk", axis=0, tiled=True)
        key_pos = jnp.arange(key_piece.shape[0], dtype=jnp.int32)

        def one_block(inputs):
            query_blk, query_pos, query_seg, run_max, run_sum, run_acc = inputs
            scores = (
                jnp.einsum(
                    "qhrd,khd->hrqk", query_blk, key_piece, preferred_element_type=jnp.float32
                )
                * scale
            )
            allowed = (key_pos[None, :] <= query_pos[:, None]) & (
                seg_piece[None, :] == query_seg[:, None]
            )
            new_max = jnp.maximum(run_max, jnp.max(jnp.where(allowed, scores, NEG), axis=-1))
            expo = jnp.where(allowed, jnp.exp(scores - new_max[..., None]), 0.0)
            decay = jnp.exp(run_max - new_max)
            new_sum = run_sum * decay + jnp.sum(expo, -1)
            new_acc = run_acc * decay[..., None] + jnp.einsum(
                "hrqk,khd->hrqd",
                expo.astype(jnp.bfloat16),
                value_piece,
                preferred_element_type=jnp.float32,
            )
            return (new_max, new_sum, new_acc)

        run_max, run_sum, run_acc = lax.map(
            one_block,
            (
                query_blocks,
                pos_blocks,
                seg_blocks,
                jnp.full((block_count, kv_here, group_size, block_rows), NEG, jnp.float32),
                jnp.zeros((block_count, kv_here, group_size, block_rows), jnp.float32),
                jnp.zeros((block_count, kv_here, group_size, block_rows, HD), jnp.float32),
            ),
        )
        attn_heads = run_acc / run_sum[..., None]
        log_total = run_max + jnp.log(run_sum)
        attn_low = (
            attn_heads.transpose(0, 3, 1, 2, 4)
            .reshape(span_len, heads_here, HD)
            .astype(jnp.bfloat16)
        )
        attn_tok = lax.all_to_all(
            attn_low, "head", split_axis=0, concat_axis=1, tiled=True
        ).reshape(tok_rows, QH * HD)
        x_mid = x_float + plain_dot(attn_tok, out_w)
        normed_two, factor_two = normalize(x_mid)
        input_two = (normed_two * gain_two_f).astype(jnp.bfloat16)
        gate_val = plain_dot(input_two, gate_w)
        up_val = plain_dot(input_two, up_w)
        sigma = jax.nn.sigmoid(gate_val)
        silu_val = gate_val * sigma
        hidden = (silu_val * up_val).astype(jnp.bfloat16)
        result = (x_mid + plain_dot(hidden, down_w)).astype(jnp.bfloat16)
        grad_down = first_dot(hidden, cot_rows)
        grad_hidden = last_dot(cot_rows, down_w)
        grad_gate_val = (grad_hidden * up_val * sigma * (1.0 + gate_val * (1.0 - sigma))).astype(
            jnp.bfloat16
        )
        grad_up_val = (grad_hidden * silu_val).astype(jnp.bfloat16)
        grad_gate_w = first_dot(input_two, grad_gate_val)
        grad_up_w = first_dot(input_two, grad_up_val)
        grad_input_two = last_dot(grad_gate_val, gate_w) + last_dot(grad_up_val, up_w)
        grad_gain_two = jnp.sum(grad_input_two * normed_two, 0)
        grad_mid = cot_rows.astype(jnp.float32) + norm_back(
            grad_input_two, gain_two_f, normed_two, factor_two
        )
        grad_branch = grad_mid.astype(jnp.bfloat16)
        grad_out_w = first_dot(attn_tok, grad_branch)
        grad_attn = last_dot(grad_branch, out_w).astype(jnp.bfloat16).reshape(tok_rows, QH, HD)
        grad_heads = lax.all_to_all(grad_attn, "head", split_axis=1, concat_axis=0, tiled=True)
        grad_blocks = grad_heads.reshape(block_count, block_rows, kv_here, group_size, HD)
        delta = jnp.sum(grad_blocks.astype(jnp.float32).transpose(0, 2, 3, 1, 4) * attn_heads, -1)
        full_k = lax.all_gather(head_k, "blk", axis=0, tiled=True)
        full_v = lax.all_gather(head_v, "blk", axis=0, tiled=True)
        full_seg = lax.all_gather(seg_rows, "blk", axis=0, tiled=True)
        key_k = full_k.reshape(cycle_count, span_len, kv_here, HD)
        key_v = full_v.reshape(cycle_count, span_len, kv_here, HD)
        key_seg = full_seg.reshape(cycle_count, span_len)
        key_pos = jnp.arange(seq_len, dtype=jnp.int32).reshape(cycle_count, span_len)

        def key_step(grad_total, key_inputs):
            blk_k, blk_v, blk_seg, blk_pos = key_inputs

            def query_step(carry, inputs):
                sum_k, sum_v = carry
                query_blk, query_pos, query_seg, lse_blk, delta_blk, grad_blk = inputs
                scores = (
                    jnp.einsum(
                        "qhrd,khd->hrqk", query_blk, blk_k, preferred_element_type=jnp.float32
                    )
                    * scale
                )
                allowed = (blk_pos[None, :] <= query_pos[:, None]) & (
                    blk_seg[None, :] == query_seg[:, None]
                )
                probs = jnp.where(allowed, jnp.exp(scores - lse_blk[..., None]), 0.0)
                grad_probs = jnp.einsum(
                    "qhrd,khd->hrqk", grad_blk, blk_v, preferred_element_type=jnp.float32
                )
                grad_scores = (probs * (grad_probs - delta_blk[..., None])).astype(jnp.bfloat16)
                grad_query = (
                    jnp.einsum(
                        "hrqk,khd->qhrd", grad_scores, blk_k, preferred_element_type=jnp.float32
                    )
                    * scale
                )
                sum_k = (
                    sum_k
                    + jnp.einsum(
                        "hrqk,qhrd->khd", grad_scores, query_blk, preferred_element_type=jnp.float32
                    )
                    * scale
                )
                sum_v = sum_v + jnp.einsum(
                    "hrqk,qhrd->khd",
                    probs.astype(jnp.bfloat16),
                    grad_blk,
                    preferred_element_type=jnp.float32,
                )
                return ((sum_k, sum_v), grad_query)

            empty_kv = jnp.zeros((span_len, kv_here, HD), jnp.float32)
            (sum_k, sum_v), grad_part = lax.scan(
                query_step,
                (empty_kv, empty_kv),
                (query_blocks, pos_blocks, seg_blocks, log_total, delta, grad_blocks),
            )
            return (grad_total + grad_part, (sum_k, sum_v))

        grad_start = jnp.zeros((block_count, block_rows, kv_here, group_size, HD), jnp.float32)
        grad_query, (sums_k, sums_v) = lax.scan(
            key_step, grad_start, (key_k, key_v, key_seg, key_pos)
        )
        sum_k = sums_k.reshape(seq_len, kv_here, HD)
        sum_v = sums_v.reshape(seq_len, kv_here, HD)
        owned_k = lax.psum_scatter(
            sum_k.astype(jnp.bfloat16), "blk", scatter_dimension=0, tiled=True
        ).astype(jnp.float32)
        owned_v = lax.psum_scatter(
            sum_v.astype(jnp.bfloat16), "blk", scatter_dimension=0, tiled=True
        ).astype(jnp.float32)
        grad_query = grad_query.reshape(span_len, heads_here, HD)
        tok_q = lax.all_to_all(
            grad_query.astype(jnp.bfloat16), "head", split_axis=0, concat_axis=1, tiled=True
        ).astype(grad_query.dtype)
        tok_k = lax.all_to_all(
            owned_k.astype(jnp.bfloat16), "head", split_axis=0, concat_axis=1, tiled=True
        ).astype(owned_k.dtype)
        tok_v = lax.all_to_all(
            owned_v.astype(jnp.bfloat16), "head", split_axis=0, concat_axis=1, tiled=True
        ).astype(owned_v.dtype)
        tok_q = tok_q.reshape(tok_rows, QH * HD).astype(jnp.bfloat16)
        tok_k = (
            jnp.sum(tok_k.reshape(tok_rows, KVH, kv_repeat, HD), 2)
            .reshape(tok_rows, KVH * HD)
            .astype(jnp.bfloat16)
        )
        tok_v = (
            jnp.sum(tok_v.reshape(tok_rows, KVH, kv_repeat, HD), 2)
            .reshape(tok_rows, KVH * HD)
            .astype(jnp.bfloat16)
        )
        grad_query_w = first_dot(input_one, tok_q)
        grad_key_w = first_dot(input_one, tok_k)
        grad_value_w = first_dot(input_one, tok_v)
        grad_input_one = (
            last_dot(tok_q, query_w) + last_dot(tok_k, key_w) + last_dot(tok_v, value_w)
        )
        grad_gain_one = jnp.sum(grad_input_one * normed_one, 0)
        grad_x = (grad_mid + norm_back(grad_input_one, gain_one_f, normed_one, factor_one)).astype(
            jnp.bfloat16
        )
        result, grad_x, terms = (
            result,
            grad_x,
            (
                grad_gain_one,
                grad_query_w,
                grad_key_w,
                grad_value_w,
                grad_out_w,
                grad_gain_two,
                grad_gate_w,
                grad_up_w,
                grad_down,
            ),
        )
        results.append(result)
        grads_x.append(grad_x)
        totals = tuple((left + right for left, right in zip(totals, terms)))
    owned = jax.tree.map(
        lambda part: part.astype(jnp.float32),
        lax.psum_scatter(shortened(totals), ("dp", "blk"), scatter_dimension=0, tiled=True),
    )
    owned = jax.tree.map(lambda part: part.astype(jnp.float32), lax.psum(shortened(owned), "head"))
    block_out = jnp.stack(results)[:, None]
    grad_input = jnp.stack(grads_x)[:, None]
    return (
        block_out,
        grad_input,
        owned[0],
        owned[1],
        owned[2],
        owned[3],
        owned[4],
        owned[5],
        owned[6],
        owned[7],
        owned[8],
    )


def solution(mesh):
    placed = (
        P(None, "dp", ("blk", "head"), None),
        P(None, "dp", "blk"),
        P(None, "dp", ("blk", "head"), None),
        P(("dp", "blk")),
        P(("dp", "blk"), None),
        P(("dp", "blk"), None),
        P(("dp", "blk"), None),
        P(("dp", "blk"), None),
        P(("dp", "blk")),
        P(("dp", "blk"), None),
        P(("dp", "blk"), None),
        P(("dp", "blk"), None),
    )
    return jax.shard_map(
        per_device,
        mesh=mesh,
        in_specs=placed,
        out_specs=(
            P(None, "dp", ("blk", "head"), None),
            P(None, "dp", ("blk", "head"), None),
            P(("dp", "blk")),
            P(("dp", "blk"), None),
            P(("dp", "blk"), None),
            P(("dp", "blk"), None),
            P(("dp", "blk"), None),
            P(("dp", "blk")),
            P(("dp", "blk"), None),
            P(("dp", "blk"), None),
            P(("dp", "blk"), None),
        ),
        check_vma=False,
    )
```

profile of v0, /device:TPU:0, one launch (start us, length us, event | category | flops | bytes accessed | tf_op | source)
XLA Modules:
  0.0 1429.7 jit_solution(12849763053035598999)
XLA Ops:
  13.7 16.3 %all-reduce.5 = (bf16[1536]{0:T(1024)(128)(2,1)S(1)}, bf16[1536]{0:T(1024)(128)(2,1)S(1)}) all-reduce(bf16[1536]{0:T(1024)(128)(2,1)S(1)} %dynamic-update-slice, bf16[1536]{0:T(1024)(128)(2,1)S(1)} %dynamic-update-slice.1), channel_id=1, replica_groups=mesh['dp'=2,'blk'=4,'head'=4] {'dp','blk'}, use_global_device_ids=true, to_apply=%add | all-reduce | flops 3072 | bytes 12288
  30.7 8.8 all-gather
  39.4 7.0 all-gather.1
  57.7 15.3 %all-gather.14.cloned.1.call-done = bf16[1536,768]{1,0:T(8,128)(2,1)} async-done(((bf16[192,768]{1,0:T(8,128)(2,1)}), bf16[1536,768]{1,0:T(8,128)(2,1)}) %all-gather.14.cloned.1.call-update) | async-done | bytes 2359312 | tf_op jit(solution)/shard_map/all_gather | solution.py:104
  105.3 13.9 all_gather.73
  119.2 14.7 %all_gather.74 = bf16[2048,2,96]{0,2,1:T(8,128)(2,1)} all-gather(bf16[512,2,96]{0,2,1:T(8,128)(2,1)S(1)} %all_to_all.220), channel_id=1, replica_groups=mesh['dp'=2,'blk'=4,'head'=4] {'blk'}, dimensions={0}, use_global_device_ids=true | all-gather | bytes 983040 | tf_op jit(solution)/shard_map/all_gather | solution.py:130
  138.0 6.3 all-to-all-start.5
  144.3 20.2 %all_gather.63 = bf16[2048,2,96]{0,2,1:T(8,128)(2,1)} all-gather(bf16[512,2,96]{0,2,1:T(8,128)(2,1)S(1)} %all_to_all.199), channel_id=1, replica_groups=mesh['dp'=2,'blk'=4,'head'=4] {'blk'}, dimensions={0}, use_global_device_ids=true | all-gather | bytes 983040 | tf_op jit(solution)/shard_map/all_gather | solution.py:129
  164.8 11.4 all_gather.66
  182.7 5.1 all-to-all-start.1
  226.8 5.3 all-to-all-start.3
  250.1 8.4 fusion.210
  258.6 55.3 %all-gather.20.cloned.1.call-done = bf16[1536,4096]{1,0:T(8,128)(2,1)} async-done(((bf16[192,4096]{1,0:T(8,128)(2,1)}), bf16[1536,4096]{1,0:T(8,128)(2,1)}) %all-gather.20.cloned.1.call-update) | async-done | bytes 12582928 | tf_op jit(solution)/shard_map/all_gather | solution.py:108
  313.9 7.7 fusion.211
  321.6 66.3 %all-gather.22.cloned.1.call-done = bf16[4096,1536]{1,0:T(8,128)(2,1)} async-done(((bf16[512,1536]{1,0:T(8,128)(2,1)}), bf16[4096,1536]{1,0:T(8,128)(2,1)}) %all-gather.22.cloned.1.call-update) | async-done | bytes 12582928 | tf_op jit(solution)/shard_map/all_gather | solution.py:109
  387.9 11.4 multiply_convert_fusion.2
  399.4 10.5 fusion.214
  409.9 11.6 multiply_reduce_fusion.1
  425.7 6.5 fusion.213
  432.2 9.9 multiply_convert_fusion
  442.1 9.8 fusion.216
  452.0 9.7 multiply_reduce_fusion
  474.4 7.1 all-to-all-done.12
  489.3 50.1 %while.25 = (s32[]{:T(128)}, f32[1,512,2,2,96]{1,4,3,2,0:T(8,128)}, bf16[4,512,2,96]{1,3,2,0:T(8,128)(2,1)}, bf16[4,512,2,96]{1,3,2,0:T(8,128)(2,1)}, bf16[4,512...) while((s32[]{:T(128)}, f32[1,512,2,2,96]{1,4,3,2,0:T(8,128)}, ...), condition=%wide.region_18.19_spmd.clone, body=%wide.region_17.18_spmd.clone.sunk | while | flops 1018593792 | bytes 67217776 | solution.py:264
  545.2 46.2 %while.24 = (s32[]{:T(128)}, f32[1,512,2,2,96]{1,4,3,2,0:T(8,128)S(1)}, bf16[4,512,2,96]{1,3,2,0:T(8,128)(2,1)}, bf16[4,512,2,96]{1,3,2,0:T(8,128)(2,1)}, bf16[4...) while((s32[]{:T(128)}, ...), condition=%wide.region_11.12_spmd.clone, body=%wide.region_10.11_spmd.clone.sunk | while | flops 1018593792 | bytes 69314976 | solution.py:264
  598.9 5.1 all-to-all-start.14
  604.0 16.3 %reduce-scatter.12.cloned.1.call-done = bf16[512,2,96]{0,2,1:T(8,128)(2,1)} async-done(((bf16[2048,2,96]{0,2,1:T(8,128)(2,1)}), bf16[512,2,96]{0,2,1:T(8,128)(2,1)}) %reduce-scatter.12.cloned.1.call-update) | async-done | bytes 196624 | tf_op jit(solution)/shard_map/reduce_scatter | solution.py:269
  627.0 8.6 all-to-all-done.10
  639.1 10.6 reduce-scatter.18.cloned.1.call-done
  656.2 22.6 %reduce-scatter.14.cloned.1.call-done = bf16[512,2,96]{0,2,1:T(8,128)(2,1)} async-done(((bf16[2048,2,96]{0,2,1:T(8,128)(2,1)}), bf16[512,2,96]{0,2,1:T(8,128)(2,1)}) %reduce-scatter.14.cloned.1.call-update) | async-done | bytes 196624 | tf_op jit(solution)/shard_map/reduce_scatter | solution.py:272
  685.4 8.6 all-to-all-done.11
  710.1 11.7 all-to-all-done.13
  725.7 12.8 all-to-all-done.9
  745.0 11.8 fusion.218
  756.8 14.7 %add_convert_fusion.2 = bf16[1536,4096]{1,0:T(8,128)(2,1)} fusion(f32[1536,4096]{1,0:T(8,128)} %fusion.218, bf16[128,1536]{1,0:T(8,128)(2,1)S(1)} %copy-done.16, bf16[128,4096]{1,0:T(8,128)(2,1)S(1)} %copy-done.37), kind=kOutput, calls=%fused_computation.80 | convolution fusion | flops 1623195648 | bytes 39190528 | tf_op jit(solution)/shard_map/dot_general | solution.py:25
  771.7 12.2 fusion.219
  783.9 16.2 %add_convert_fusion.1 = bf16[1536,4096]{1,0:T(8,128)(2,1)} fusion(f32[1536,4096]{1,0:T(8,128)} %fusion.219, bf16[128,1536]{1,0:T(8,128)(2,1)S(1)} %copy-done.16, bf16[128,4096]{1,0:T(8,128)(2,1)S(1)} %copy-done.35), kind=kOutput, calls=%fused_computation.79 | convolution fusion | flops 1623195648 | bytes 39190528 | tf_op jit(solution)/shard_map/dot_general | solution.py:25
  801.2 11.9 fusion.165
  813.2 15.4 %add_convert_fusion = bf16[4096,1536]{1,0:T(8,128)(2,1)} fusion(f32[4096,1536]{1,0:T(8,128)} %fusion.165, bf16[128,4096]{1,0:T(8,128)(2,1)S(1)} %copy-done.25, bf16[2,1,128,1536]{3,2,1,0:T(8,128)(2,1)S(1)} %copy-done.45), kind=kOutput, calls=%fused_computation.78 | convolution fusion | flops 1623195648 | bytes 39190528 | tf_op jit(solution)/shard_map/dot_general | solution.py:25
  829.1 57.6 %reduce-scatter.20.cloned.1.call-done = bf16[192,1536]{1,0:T(8,128)(2,1)} async-done(((bf16[1536,1536]{1,0:T(8,128)(2,1)}), bf16[192,1536]{1,0:T(8,128)(2,1)}) %reduce-scatter.20.cloned.1.call-update) | async-done | bytes 589840 | tf_op jit(solution)/shard_map/reduce_scatter | solution.py:326
  886.7 95.8 %reduce-scatter.28.cloned.1.call-done = bf16[192,4096]{1,0:T(8,128)(2,1)} async-done(((bf16[1536,4096]{1,0:T(8,128)(2,1)}), bf16[192,4096]{1,0:T(8,128)(2,1)}) %reduce-scatter.28.cloned.1.call-update) | async-done | bytes 1572880 | tf_op jit(solution)/shard_map/reduce_scatter | solution.py:326
  982.4 95.8 %reduce-scatter.30.cloned.1.call-done = bf16[192,4096]{1,0:T(8,128)(2,1)} async-done(((bf16[1536,4096]{1,0:T(8,128)(2,1)}), bf16[192,4096]{1,0:T(8,128)(2,1)}) %reduce-scatter.30.cloned.1.call-update) | async-done | bytes 1572880 | tf_op jit(solution)/shard_map/reduce_scatter | solution.py:326
  1078.2 95.8 %reduce-scatter.32.cloned.1.call-done = bf16[512,1536]{1,0:T(8,128)(2,1)} async-done(((bf16[4096,1536]{1,0:T(8,128)(2,1)}), bf16[512,1536]{1,0:T(8,128)(2,1)}) %reduce-scatter.32.cloned.1.call-update) | async-done | bytes 1572880 | tf_op jit(solution)/shard_map/reduce_scatter | solution.py:326
  1174.7 6.5 fusion.96
  1181.3 7.6 fusion.97
  1198.1 14.9 %all-reduce.4 = (bf16[1536]{0:T(1024)(128)(2,1)S(1)}, bf16[1536]{0:T(1024)(128)(2,1)S(1)}) all-reduce(bf16[1536]{0:T(1024)(128)(2,1)S(1)} %add_convert_fusion.6, bf16[1536]{0:T(1024)(128)(2,1)S(1)} %add_convert_fusion.5), channel_id=8, replica_groups=mesh['dp'=2,'blk'=4,'head'=4] {'dp','blk'}, use_global_device_ids=true, to_apply=%region_24.25.clone | all-reduce | flops 3072 | bytes 12288
  1213.2 12.1 all-reduce.6
  1229.1 179.4 %all-reduce.10.cloned.1.call-done = (bf16[192,1536]{1,0:T(8,128)(2,1)}, bf16[192,768]{1,0:T(8,128)(2,1)}, bf16[192,768]{1,0:T(8,128)(2,1)}, bf16[192,1536]{1,0:T...) async-done(((bf16[192,1536]{1,0:T(8,128)(2,1)}, bf16[192,768]{1,0:T(8,128)(2,1)}, bf16[192,768]{1,0:T(8,128)(2,1)}, ...) | async-done | bytes 6488080 | tf_op jit(solution)/shard_map/psum | solution.py:328
  (551 shorter events, 328.6 us)
Async XLA Ops:
  7.2 39.2 %copy-start.6 = (bf16[2,1,128,1536]{3,2,1,0:T(8,128)(2,1)S(1)}, bf16[2,1,128,1536]{3,2,1,0:T(8,128)(2,1)}, u32[]{:S(2)}) copy-start(bf16[2,1,128,1536]{3,2,1,0:T(8,128)(2,1)} %param.16) | copy-start | bytes 2359300
  7.2 42.5 %all-gather.10.cloned.1.call-start = ((), (), s32[]{:S(2)}) async-start(), calls=%async_computation.27 | async-start | bytes 2654208 | tf_op jit(solution)/shard_map/all_gather | solution.py:103
  8.0 65.1 %all-gather.14.cloned.1.call-start = ((), (), s32[]{:S(2)}) async-start(), calls=%async_computation.29 | async-start | bytes 2654208 | tf_op jit(solution)/shard_map/all_gather | solution.py:104
  8.7 125.2 %all-gather.12.cloned.1.call-start = ((), (), s32[]{:S(2)}) async-start(), calls=%async_computation.28 | async-start | bytes 5308416 | tf_op jit(solution)/shard_map/all_gather | solution.py:102
  9.5 234.9 %all-gather.16.cloned.1.call-start = ((), (), s32[]{:S(2)}) async-start(), calls=%async_computation.30 | async-start | bytes 5308416 | tf_op jit(solution)/shard_map/all_gather | solution.py:105
  10.0 240.1 %all-gather.18.cloned.1.call-start = ((), (), s32[]{:S(2)}) async-start(), calls=%async_computation.31 | async-start | bytes 14155776 | tf_op jit(solution)/shard_map/all_gather | solution.py:107
  10.6 303.3 %all-gather.20.cloned.1.call-start = ((), (), s32[]{:S(2)}) async-start(), calls=%async_computation.32 | async-start | bytes 14155776 | tf_op jit(solution)/shard_map/all_gather | solution.py:108
  11.2 376.8 %all-gather.22.cloned.1.call-start = ((), (), s32[]{:S(2)}) async-start(), calls=%async_computation.33 | async-start | bytes 14155776 | tf_op jit(solution)/shard_map/all_gather | solution.py:109
  30.1 146.1 %copy-start.73 = (f32[1536]{0:T(1024)}, f32[1536]{0:T(1024)S(1)}, u32[]{:S(2)}) copy-start(f32[1536]{0:T(1024)S(1)} %convert_element_type.334) | copy-start | bytes 18436
  46.7 87.2 %copy-start.81 = (f32[128]{0:T(128)}, f32[128]{0:T(128)S(1)}, u32[]{:S(2)}) copy-start(f32[128]{0:T(128)S(1)} %get-tuple-element.729) | copy-start | bytes 1540
  46.7 129.5 %copy-start.77 = (f32[128]{0:T(128)}, f32[128]{0:T(128)S(1)}, u32[]{:S(2)}) copy-start(f32[128]{0:T(128)S(1)} %get-tuple-element.730) | copy-start | bytes 1540
  52.8 25.0 %all-to-all-start.4 = ((bf16[128,8,96]{0,2,1:T(8,128)(2,1)}), bf16[128,8,96]{0,2,1:T(8,128)(2,1)S(1)}, u32[]{:S(2)}, u32[]{:S(2)}) async-start(bf16[128,8,96]{0,2,1:T(8,128)(2,1)} %bitcast.29), calls=%async_computation.4 | async-start | bytes 393216 | tf_op jit(solution)/shard_map/all_to_all | solution.py:122
  77.8 12.6 all-to-all-start.6
  90.5 10.3 all-to-all-start
  100.8 37.3 %all-to-all-start.2 = ((bf16[128,8,96]{0,2,1:T(8,128)(2,1)}), bf16[128,8,96]{0,2,1:T(8,128)(2,1)S(1)}, u32[]{:S(2)}, u32[]{:S(2)}) async-start(bf16[128,8,96]{0,2,1:T(8,128)(2,1)} %bitcast.13), calls=%async_computation.2 | async-start | bytes 393216 | tf_op jit(solution)/shard_map/all_to_all | solution.py:123
  119.2 70.9 %copy-start.52 = (bf16[2048,2,96]{0,2,1:T(8,128)(2,1)}, bf16[2048,2,96]{0,2,1:T(8,128)(2,1)S(1)}, u32[]{:S(2)}) copy-start(bf16[2048,2,96]{0,2,1:T(8,128)(2,1)S(1)} %all_gather.73) | copy-start | bytes 2359300
  138.0 44.7 %all-to-all-start.5 = ((bf16[128,16,96]{0,2,1:T(8,128)(2,1)}), bf16[128,16,96]{0,2,1:T(8,128)(2,1)S(1)}, u32[]{:S(2)}, u32[]{:S(2)}) async-start(bf16[128,16,96]{0,2,1:T(8,128)(2,1)} %bitcast.34), calls=%async_computation.5 | async-start | bytes 786432 | tf_op jit(solution)/shard_map/all_to_all | solution.py:121
  182.7 22.0 %all-to-all-start.1 = ((bf16[128,16,96]{0,2,1:T(8,128)(2,1)}), bf16[128,16,96]{0,2,1:T(8,128)(2,1)}, u32[]{:S(2)}, u32[]{:S(2)}) async-start(bf16[128,16,96]{0,2,1:T(8,128)(2,1)} %bitcast.9), calls=%async_computation.1 | async-start | bytes 786432 | tf_op jit(solution)/shard_map/all_to_all | solution.py:121
  204.7 22.1 %all-to-all-start.7 = ((bf16[512,4,96]{2,1,0:T(4,128)(2,1)}), bf16[512,4,96]{2,1,0:T(4,128)(2,1)S(1)}, u32[]{:S(2)}, u32[]{:S(2)}) async-start(bf16[512,4,96]{2,1,0:T(4,128)(2,1)} %copy.196), calls=%async_computation.7 | async-start | bytes 1048576 | tf_op jit(solution)/shard_map/all_to_all | solution.py:175
  226.8 16.0 %all-to-all-start.3 = ((bf16[512,4,96]{2,1,0:T(4,128)(2,1)}), bf16[512,4,96]{2,1,0:T(4,128)(2,1)}, u32[]{:S(2)}, u32[]{:S(2)}) async-start(bf16[512,4,96]{2,1,0:T(4,128)(2,1)} %copy.186), calls=%async_computation.3 | async-start | bytes 1048576 | tf_op jit(solution)/shard_map/all_to_all | solution.py:175
  250.1 63.8 %copy-start.17 = (bf16[128,1536]{1,0:T(8,128)(2,1)}, bf16[128,1536]{1,0:T(8,128)(2,1)S(1)}, u32[]{:S(2)}) copy-start(bf16[128,1536]{1,0:T(8,128)(2,1)S(1)} %multiply_convert_fusion.7) | copy-start | bytes 1179652
  258.6 129.4 %copy-start.43 = (bf16[2,1,128,1536]{3,2,1,0:T(8,128)(2,1)S(1)}, bf16[2,1,128,1536]{3,2,1,0:T(8,128)(2,1)}, u32[]{:S(2)}) copy-start(bf16[2,1,128,1536]{3,2,1,0:T(8,128)(2,1)} %param.18) | copy-start | bytes 2359300
  464.8 16.7 %all-to-all-start.12 = ((bf16[128,16,96]{0,2,1:T(8,128)(2,1)}), bf16[128,16,96]{0,2,1:T(8,128)(2,1)S(1)}, u32[]{:S(2)}, u32[]{:S(2)}) async-start(bf16[128,16,96]{0,2,1:T(8,128)(2,1)} %bitcast.78), calls=%async_computation.14 | async-start | bytes 786432 | tf_op jit(solution)/shard_map/all_to_all | solution.py:203
  481.5 60.2 %all-to-all-start.8 = ((bf16[128,16,96]{0,2,1:T(8,128)(2,1)}), bf16[128,16,96]{0,2,1:T(8,128)(2,1)}, u32[]{:S(2)}, u32[]{:S(2)}) async-start(bf16[128,16,96]{0,2,1:T(8,128)(2,1)} %bitcast.57), calls=%async_computation.8 | async-start | bytes 786432 | tf_op jit(solution)/shard_map/all_to_all | solution.py:203
  485.6 111.4 %reduce-scatter.16.cloned.1.call-start = ((), (), s32[]{:S(2)}) async-start(), calls=%async_computation.36 | async-start | bytes 983040 | tf_op jit(solution)/shard_map/reduce_scatter | solution.py:269
  541.7 78.7 %reduce-scatter.12.cloned.1.call-start = ((), (), s32[]{:S(2)}) async-start(), calls=%async_computation.34 | async-start | bytes 983040 | tf_op jit(solution)/shard_map/reduce_scatter | solution.py:269
  593.7 56.1 %reduce-scatter.18.cloned.1.call-start = ((), (), s32[]{:S(2)}) async-start(), calls=%async_computation.37 | async-start | bytes 983040 | tf_op jit(solution)/shard_map/reduce_scatter | solution.py:272
  593.8 42.1 %copy-start.7 = (bf16[2,1,128,1536]{3,2,1,0:T(8,128)(2,1)S(1)}, bf16[2,1,128,1536]{3,2,1,0:T(8,128)(2,1)}, u32[]{:S(2)}) copy-start(bf16[2,1,128,1536]{3,2,1,0:T(8,128)(2,1)} %param.16) | copy-start | bytes 2359300
  593.8 42.1 %copy-start.74 = (f32[1536]{0:T(1024)S(1)}, f32[1536]{0:T(1024)}, u32[]{:S(2)}) copy-start(f32[1536]{0:T(1024)} %copy-done.73) | copy-start | bytes 18436
  593.8 42.1 %copy-start.78 = (f32[128]{0:T(128)S(1)}, f32[128]{0:T(128)}, u32[]{:S(2)}) copy-start(f32[128]{0:T(128)} %copy-done.77) | copy-start | bytes 1540
  596.0 82.8 %reduce-scatter.14.cloned.1.call-start = ((), (), s32[]{:S(2)}) async-start(), calls=%async_computation.35 | async-start | bytes 983040 | tf_op jit(solution)/shard_map/reduce_scatter | solution.py:272
  598.9 23.3 %all-to-all-start.14 = ((bf16[512,2,96]{2,1,0:T(2,128)(2,1)}), bf16[512,2,96]{2,1,0:T(2,128)(2,1)S(1)}, u32[]{:S(2)}, u32[]{:S(2)}) async-start(bf16[512,2,96]{2,1,0:T(2,128)(2,1)} %copy.222), calls=%async_computation.17 | async-start | bytes 524288 | tf_op jit(solution)/shard_map/all_to_all | solution.py:279
  622.2 13.5 all-to-all-start.10
  626.7 202.2 %reduce-scatter.22.cloned.1.call-start = ((), (), s32[]{:S(2)}) async-start(), calls=%async_computation.39 | async-start | bytes 2654208 | tf_op jit(solution)/shard_map/reduce_scatter | solution.py:326
  651.6 29.0 %all-to-all-start.15 = ((bf16[512,2,96]{2,1,0:T(2,128)(2,1)}), bf16[512,2,96]{2,1,0:T(2,128)(2,1)S(1)}, u32[]{:S(2)}, u32[]{:S(2)}) async-start(bf16[512,2,96]{2,1,0:T(2,128)(2,1)} %copy.226), calls=%async_computation.19 | async-start | bytes 524288 | tf_op jit(solution)/shard_map/all_to_all | solution.py:282
  680.6 13.5 all-to-all-start.11
  685.2 143.8 %reduce-scatter.24.cloned.1.call-start = ((), (), s32[]{:S(2)}) async-start(), calls=%async_computation.40 | async-start | bytes 2654208 | tf_op jit(solution)/shard_map/reduce_scatter | solution.py:326
  697.6 131.5 %reduce-scatter.26.cloned.1.call-start = ((), (), s32[]{:S(2)}) async-start(), calls=%async_computation.41 | async-start | bytes 5308416 | tf_op jit(solution)/shard_map/reduce_scatter | solution.py:326
  705.5 16.4 %all-to-all-start.13 = ((bf16[512,4,96]{2,1,0:T(4,128)(2,1)}), bf16[512,4,96]{2,1,0:T(4,128)(2,1)S(1)}, u32[]{:S(2)}, u32[]{:S(2)}) async-start(bf16[512,4,96]{2,1,0:T(4,128)(2,1)} %bitcast.83), calls=%async_computation.15 | async-start | bytes 1048576 | tf_op jit(solution)/shard_map/all_to_all | solution.py:276
  721.9 16.6 %all-to-all-start.9 = ((bf16[512,4,96]{2,1,0:T(4,128)(2,1)}), bf16[512,4,96]{2,1,0:T(4,128)(2,1)S(1)}, u32[]{:S(2)}, u32[]{:S(2)}) async-start(bf16[512,4,96]{2,1,0:T(4,128)(2,1)} %bitcast.62), calls=%async_computation.9 | async-start | bytes 1048576 | tf_op jit(solution)/shard_map/all_to_all | solution.py:276
  725.4 161.3 %reduce-scatter.20.cloned.1.call-start = ((), (), s32[]{:S(2)}) async-start(), calls=%async_computation.38 | async-start | bytes 5308416 | tf_op jit(solution)/shard_map/reduce_scatter | solution.py:326
  744.0 238.4 %reduce-scatter.28.cloned.1.call-start = ((), (), s32[]{:S(2)}) async-start(), calls=%async_computation.42 | async-start | bytes 14155776 | tf_op jit(solution)/shard_map/reduce_scatter | solution.py:326
  771.5 306.7 %reduce-scatter.30.cloned.1.call-start = ((), (), s32[]{:S(2)}) async-start(), calls=%async_computation.43 | async-start | bytes 14155776 | tf_op jit(solution)/shard_map/reduce_scatter | solution.py:326
  800.1 373.9 %reduce-scatter.32.cloned.1.call-start = ((), (), s32[]{:S(2)}) async-start(), calls=%async_computation.44 | async-start | bytes 14155776 | tf_op jit(solution)/shard_map/reduce_scatter | solution.py:326
  828.6 346.0 %copy-start.79 = (f32[1536]{0:T(1024)S(1)}, f32[1536]{0:T(1024)}, u32[]{:S(2)}) copy-start(f32[1536]{0:T(1024)} %get-tuple-element.608) | copy-start | bytes 18436
  828.7 346.0 %copy-start.80 = (f32[1536]{0:T(1024)S(1)}, f32[1536]{0:T(1024)}, u32[]{:S(2)}) copy-start(f32[1536]{0:T(1024)} %get-tuple-element.606) | copy-start | bytes 18436
  828.7 346.0 %copy-start.11 = (f32[128,1536]{1,0:T(8,128)S(1)}, f32[128,1536]{1,0:T(8,128)}, u32[]{:S(2)}) copy-start(f32[128,1536]{1,0:T(8,128)} %get-tuple-element.725) | copy-start | bytes 2359300
  828.7 579.8 %all-reduce.10.cloned.1.call-start = ((), (), s32[]{:S(2)}) async-start(), calls=%async_computation.45 | async-start | bytes 12976128 | tf_op jit(solution)/shard_map/psum | solution.py:328
  (123 other events, 775.2 us)
Sparse Core Ops, SparseCore 0:
  9.9 32.1 all-gather.9
  44.0 28.9 all-gather.13
  75.0 42.0 all-gather.11
  118.8 46.9 all-gather.15
  167.5 72.4 all-gather.17
  241.7 72.1 all-gather.19
  315.8 72.1 all-gather.21
  541.8 26.5 reduce-scatter.15
  593.8 26.4 reduce-scatter.11
  623.7 26.0 reduce-scatter.17
  652.7 26.0 reduce-scatter.13
  682.6 42.4 reduce-scatter.21
  729.4 42.4 reduce-scatter.23
  775.2 53.8 reduce-scatter.25
  832.8 53.8 reduce-scatter.19
  890.0 92.3 reduce-scatter.27
  985.8 92.3 reduce-scatter.29
  1081.6 92.3 reduce-scatter.31
  1176.9 231.5 all-reduce.9
where the time goes:
time: 1440 us; the launch traced here: 1430 us
  waiting for transfers between devices  770 us (53%)
  matrix products  342 us (24%)
  blocking collectives  119 us (8%)
  starting transfers between devices  74.8 us (5%)
  local copies, waits for them, and re-layouts  70.3 us (5%)
  other arithmetic  35.4 us (2%)
  between operations  16.9 us (1%)
    reduce_scatter x7, waiting for transfers between devices, per_device(): lax.psum_scatter(shortened(totals), ('dp', 'blk'), scatter_dimension=0, t...  345 us
    psum x1, waiting for transfers between devices, per_device(): lax.psum(shortened(owned), 'head')  179 us
    dot_general x14, matrix products, first_dot(): lax.dot_general(left, right, (((0,), (0,)), ((), ())), preferred_element_...  98.8 us
    dot_general x14, matrix products, last_dot(): lax.dot_general(left, right, (((1,), (1,)), ((), ())), preferred_element_...  76.6 us
    all_gather x1, waiting for transfers between devices, per_device(): down_w = lax.all_gather(shards[8], ('dp', 'blk'), axis=0, tiled=True)  66.3 us
    dot_general x14, matrix products, plain_dot(): return jnp.dot(left, right, preferred_element_type=jnp.float32)  63.4 us
    all_gather x1, waiting for transfers between devices, per_device(): up_w = lax.all_gather(shards[7], ('dp', 'blk'), axis=0, tiled=True)  55.3 us
    all_gather x2, blocking collectives, per_device(): key_piece = lax.all_gather(head_k, 'blk', axis=0, tiled=True)  34.2 us
  transfers between devices with their start and end apart: 35, of which 19 were waited for; matrix products, arithmetic and copies ran while one was open for 24% of the time, Pallas kernels for 0%

commit v1 on v0

--- a/solution.py
+++ b/solution.py
@@ -273,8 +273,16 @@
             sum_v.astype(jnp.bfloat16), "blk", scatter_dimension=0, tiled=True
         ).astype(jnp.float32)
         grad_query = grad_query.reshape(span_len, heads_here, HD)
-        tok_q = lax.all_to_all(
-            grad_query.astype(jnp.bfloat16), "head", split_axis=0, concat_axis=1, tiled=True
+        tok_q = jnp.concatenate(
+            lax.all_to_all(
+                jnp.stack(
+                    jnp.split(grad_query.astype(jnp.bfloat16), lax.axis_size("head"), axis=0)
+                ),
+                "head",
+                0,
+                0,
+            ),
+            axis=1,
         ).astype(grad_query.dtype)
         tok_k = lax.all_to_all(
             owned_k.astype(jnp.bfloat16), "head", split_axis=0, concat_axis=1, tiled=True

time: 1440 us -> 1440 us (level)
  transfers between devices with their start and end apart: 35 -> 35, of which waited for: 19 -> 19; matrix products, arithmetic and copies ran while one was open for 24% -> 25% of each run, Pallas kernels for 0% -> 0%
where the time goes in v1:
time: 1440 us; the launch traced here: 1430 us
  waiting for transfers between devices  765 us (53%)
  matrix products  349 us (24%)
  blocking collectives  119 us (8%)
  starting transfers between devices  74.9 us (5%)
  local copies, waits for them, and re-layouts  66.4 us (5%)
  other arithmetic  37 us (3%)
  between operations  17 us (1%)
    reduce_scatter x7, waiting for transfers between devices, per_device(): lax.psum_scatter(shortened(totals), ('dp', 'blk'), scatter_dimension=0, t...  351 us
    psum x1, waiting for transfers between devices, per_device(): lax.psum(shortened(owned), 'head')  179 us
    dot_general x14, matrix products, first_dot(): lax.dot_general(left, right, (((0,), (0,)), ((), ())), preferred_element_...  106 us
    dot_general x14, matrix products, last_dot(): lax.dot_general(left, right, (((1,), (1,)), ((), ())), preferred_element_...  76.6 us
    all_gather x1, waiting for transfers between devices, per_device(): down_w = lax.all_gather(shards[8], ('dp', 'blk'), axis=0, tiled=True)  66.3 us
    dot_general x14, matrix products, plain_dot(): return jnp.dot(left, right, preferred_element_type=jnp.float32)  63.4 us
    all_gather x1, waiting for transfers between devices, per_device(): up_w = lax.all_gather(shards[7], ('dp', 'blk'), axis=0, tiled=True)  55.4 us
    all_gather x2, blocking collectives, per_device(): key_piece = lax.all_gather(head_k, 'blk', axis=0, tiled=True)  34.1 us
  transfers between devices with their start and end apart: 35, of which 19 were waited for; matrix products, arithmetic and copies ran while one was open for 25% of the time, Pallas kernels for 0%

profile of v1, /device:TPU:0, one launch (start us, length us, event | category | flops | bytes accessed | tf_op | source)
XLA Modules:
  0.0 1429.8 jit_solution(1590820496180316066)
XLA Ops:
  13.7 16.3 %all-reduce.5 = (bf16[1536]{0:T(1024)(128)(2,1)S(1)}, bf16[1536]{0:T(1024)(128)(2,1)S(1)}) all-reduce(bf16[1536]{0:T(1024)(128)(2,1)S(1)} %dynamic-update-slice, bf16[1536]{0:T(1024)(128)(2,1)S(1)} %dynamic-update-slice.1), channel_id=1, replica_groups=mesh['dp'=2,'blk'=4,'head'=4] {'dp','blk'}, use_global_device_ids=true, to_apply=%add | all-reduce | flops 3072 | bytes 12288
  30.7 8.8 all-gather
  39.4 7.0 all-gather.1
  57.7 15.3 %all-gather.14.cloned.1.call-done = bf16[1536,768]{1,0:T(8,128)(2,1)} async-done(((bf16[192,768]{1,0:T(8,128)(2,1)}), bf16[1536,768]{1,0:T(8,128)(2,1)}) %all-gather.14.cloned.1.call-update) | async-done | bytes 2359312 | tf_op jit(solution)/shard_map/all_gather | solution.py:104
  105.3 13.9 all_gather.73
  119.3 14.7 %all_gather.74 = bf16[2048,2,96]{0,2,1:T(8,128)(2,1)} all-gather(bf16[512,2,96]{0,2,1:T(8,128)(2,1)S(1)} %all_to_all.200), channel_id=1, replica_groups=mesh['dp'=2,'blk'=4,'head'=4] {'blk'}, dimensions={0}, use_global_device_ids=true | all-gather | bytes 983040 | tf_op jit(solution)/shard_map/all_gather | solution.py:130
  138.0 6.4 all-to-all-start.5
  144.5 20.2 %all_gather.63 = bf16[2048,2,96]{0,2,1:T(8,128)(2,1)} all-gather(bf16[512,2,96]{0,2,1:T(8,128)(2,1)S(1)} %all_to_all.179), channel_id=1, replica_groups=mesh['dp'=2,'blk'=4,'head'=4] {'blk'}, dimensions={0}, use_global_device_ids=true | all-gather | bytes 983040 | tf_op jit(solution)/shard_map/all_gather | solution.py:129
  164.9 11.3 all_gather.66
  226.9 5.3 all-to-all-start.3
  250.2 8.4 fusion.212
  258.6 55.4 %all-gather.20.cloned.1.call-done = bf16[1536,4096]{1,0:T(8,128)(2,1)} async-done(((bf16[192,4096]{1,0:T(8,128)(2,1)}), bf16[1536,4096]{1,0:T(8,128)(2,1)}) %all-gather.20.cloned.1.call-update) | async-done | bytes 12582928 | tf_op jit(solution)/shard_map/all_gather | solution.py:108
  314.0 7.7 fusion.213
  321.7 66.3 %all-gather.22.cloned.1.call-done = bf16[4096,1536]{1,0:T(8,128)(2,1)} async-done(((bf16[512,1536]{1,0:T(8,128)(2,1)}), bf16[4096,1536]{1,0:T(8,128)(2,1)}) %all-gather.22.cloned.1.call-update) | async-done | bytes 12582928 | tf_op jit(solution)/shard_map/all_gather | solution.py:109
  388.0 11.4 multiply_convert_fusion.2
  399.4 10.5 fusion.216
  410.0 11.6 multiply_reduce_fusion.1
  425.8 6.5 fusion.215
  432.3 9.9 multiply_convert_fusion
  442.2 9.8 fusion.218
  452.1 9.8 multiply_reduce_fusion
  474.5 7.1 all-to-all-done.12
  489.4 50.1 %while.25 = (s32[]{:T(128)}, f32[1,512,2,2,96]{1,4,3,2,0:T(8,128)}, bf16[4,512,2,96]{1,3,2,0:T(8,128)(2,1)}, bf16[4,512,2,96]{1,3,2,0:T(8,128)(2,1)}, bf16[4,512...) while((s32[]{:T(128)}, f32[1,512,2,2,96]{1,4,3,2,0:T(8,128)}, ...), condition=%wide.region_18.19_spmd.clone, body=%wide.region_17.18_spmd.clone.sunk | while | flops 1018593792 | bytes 67217776 | solution.py:264
  545.3 46.3 %while.24 = (s32[]{:T(128)}, f32[1,512,2,2,96]{1,4,3,2,0:T(8,128)S(1)}, bf16[4,512,2,96]{1,3,2,0:T(8,128)(2,1)}, bf16[4,512,2,96]{1,3,2,0:T(8,128)(2,1)}, bf16[4...) while((s32[]{:T(128)}, ...), condition=%wide.region_11.12_spmd.clone, body=%wide.region_10.11_spmd.clone.sunk | while | flops 1018593792 | bytes 69314976 | solution.py:264
  604.1 16.3 %reduce-scatter.12.cloned.1.call-done = bf16[512,2,96]{0,2,1:T(8,128)(2,1)} async-done(((bf16[2048,2,96]{0,2,1:T(8,128)(2,1)}), bf16[512,2,96]{0,2,1:T(8,128)(2,1)}) %reduce-scatter.12.cloned.1.call-update) | async-done | bytes 196624 | tf_op jit(solution)/shard_map/reduce_scatter | solution.py:269
  627.1 8.6 all-to-all-done.10
  639.3 10.6 reduce-scatter.18.cloned.1.call-done
  656.3 22.6 %reduce-scatter.14.cloned.1.call-done = bf16[512,2,96]{0,2,1:T(8,128)(2,1)} async-done(((bf16[2048,2,96]{0,2,1:T(8,128)(2,1)}), bf16[512,2,96]{0,2,1:T(8,128)(2,1)}) %reduce-scatter.14.cloned.1.call-update) | async-done | bytes 196624 | tf_op jit(solution)/shard_map/reduce_scatter | solution.py:272
  685.6 8.6 all-to-all-done.11
  708.5 9.4 all-to-all-done.9
  721.4 5.2 fusion.196
  731.2 7.4 fusion.90
  739.6 11.8 fusion.220
  751.4 14.9 %add_convert_fusion.2 = bf16[1536,4096]{1,0:T(8,128)(2,1)} fusion(f32[1536,4096]{1,0:T(8,128)} %fusion.220, bf16[128,1536]{1,0:T(8,128)(2,1)S(1)} %copy-done.16, bf16[128,4096]{1,0:T(8,128)(2,1)S(1)} %copy-done.37), kind=kOutput, calls=%fused_computation.80 | convolution fusion | flops 1623195648 | bytes 39190528 | tf_op jit(solution)/shard_map/dot_general | solution.py:25
  766.6 11.5 fusion.221
  778.1 16.7 %add_convert_fusion.1 = bf16[1536,4096]{1,0:T(8,128)(2,1)} fusion(f32[1536,4096]{1,0:T(8,128)} %fusion.221, bf16[128,1536]{1,0:T(8,128)(2,1)S(1)} %copy-done.16, bf16[128,4096]{1,0:T(8,128)(2,1)S(1)} %copy-done.35), kind=kOutput, calls=%fused_computation.79 | convolution fusion | flops 1623195648 | bytes 39190528 | tf_op jit(solution)/shard_map/dot_general | solution.py:25
  796.0 11.8 fusion.165
  807.8 15.0 %add_convert_fusion = bf16[4096,1536]{1,0:T(8,128)(2,1)} fusion(f32[4096,1536]{1,0:T(8,128)} %fusion.165, bf16[128,4096]{1,0:T(8,128)(2,1)S(1)} %copy-done.25, bf16[2,1,128,1536]{3,2,1,0:T(8,128)(2,1)S(1)} %copy-done.45), kind=kOutput, calls=%fused_computation.78 | convolution fusion | flops 1623195648 | bytes 39190528 | tf_op jit(solution)/shard_map/dot_general | solution.py:25
  823.1 6.1 reduce-scatter.26.cloned.1.call-done
  829.2 57.6 %reduce-scatter.20.cloned.1.call-done = bf16[192,1536]{1,0:T(8,128)(2,1)} async-done(((bf16[1536,1536]{1,0:T(8,128)(2,1)}), bf16[192,1536]{1,0:T(8,128)(2,1)}) %reduce-scatter.20.cloned.1.call-update) | async-done | bytes 589840 | tf_op jit(solution)/shard_map/reduce_scatter | solution.py:334
  886.8 95.8 %reduce-scatter.28.cloned.1.call-done = bf16[192,4096]{1,0:T(8,128)(2,1)} async-done(((bf16[1536,4096]{1,0:T(8,128)(2,1)}), bf16[192,4096]{1,0:T(8,128)(2,1)}) %reduce-scatter.28.cloned.1.call-update) | async-done | bytes 1572880 | tf_op jit(solution)/shard_map/reduce_scatter | solution.py:334
  982.6 95.8 %reduce-scatter.30.cloned.1.call-done = bf16[192,4096]{1,0:T(8,128)(2,1)} async-done(((bf16[1536,4096]{1,0:T(8,128)(2,1)}), bf16[192,4096]{1,0:T(8,128)(2,1)}) %reduce-scatter.30.cloned.1.call-update) | async-done | bytes 1572880 | tf_op jit(solution)/shard_map/reduce_scatter | solution.py:334
  1078.4 95.8 %reduce-scatter.32.cloned.1.call-done = bf16[512,1536]{1,0:T(8,128)(2,1)} async-done(((bf16[4096,1536]{1,0:T(8,128)(2,1)}), bf16[512,1536]{1,0:T(8,128)(2,1)}) %reduce-scatter.32.cloned.1.call-update) | async-done | bytes 1572880 | tf_op jit(solution)/shard_map/reduce_scatter | solution.py:334
  1174.9 6.5 fusion.96
  1181.5 7.6 fusion.97
  1198.3 14.9 %all-reduce.4 = (bf16[1536]{0:T(1024)(128)(2,1)S(1)}, bf16[1536]{0:T(1024)(128)(2,1)S(1)}) all-reduce(bf16[1536]{0:T(1024)(128)(2,1)S(1)} %add_convert_fusion.6, bf16[1536]{0:T(1024)(128)(2,1)S(1)} %add_convert_fusion.5), channel_id=8, replica_groups=mesh['dp'=2,'blk'=4,'head'=4] {'dp','blk'}, use_global_device_ids=true, to_apply=%region_24.25.clone | all-reduce | flops 3072 | bytes 12288
  1213.3 12.2 all-reduce.6
  1229.2 179.4 %all-reduce.10.cloned.1.call-done = (bf16[192,1536]{1,0:T(8,128)(2,1)}, bf16[192,768]{1,0:T(8,128)(2,1)}, bf16[192,768]{1,0:T(8,128)(2,1)}, bf16[192,1536]{1,0:T...) async-done(((bf16[192,1536]{1,0:T(8,128)(2,1)}, bf16[192,768]{1,0:T(8,128)(2,1)}, bf16[192,768]{1,0:T(8,128)(2,1)}, ...) | async-done | bytes 6488080 | tf_op jit(solution)/shard_map/psum | solution.py:336
  (551 shorter events, 335.9 us)
Async XLA Ops:
  7.2 39.2 %copy-start.6 = (bf16[2,1,128,1536]{3,2,1,0:T(8,128)(2,1)S(1)}, bf16[2,1,128,1536]{3,2,1,0:T(8,128)(2,1)}, u32[]{:S(2)}) copy-start(bf16[2,1,128,1536]{3,2,1,0:T(8,128)(2,1)} %param.16) | copy-start | bytes 2359300
  7.2 42.5 %all-gather.10.cloned.1.call-start = ((), (), s32[]{:S(2)}) async-start(), calls=%async_computation.27 | async-start | bytes 2654208 | tf_op jit(solution)/shard_map/all_gather | solution.py:103
  8.0 65.1 %all-gather.14.cloned.1.call-start = ((), (), s32[]{:S(2)}) async-start(), calls=%async_computation.29 | async-start | bytes 2654208 | tf_op jit(solution)/shard_map/all_gather | solution.py:104
  8.7 125.2 %all-gather.12.cloned.1.call-start = ((), (), s32[]{:S(2)}) async-start(), calls=%async_computation.28 | async-start | bytes 5308416 | tf_op jit(solution)/shard_map/all_gather | solution.py:102
  9.5 234.9 %all-gather.16.cloned.1.call-start = ((), (), s32[]{:S(2)}) async-start(), calls=%async_computation.30 | async-start | bytes 5308416 | tf_op jit(solution)/shard_map/all_gather | solution.py:105
  10.0 240.1 %all-gather.18.cloned.1.call-start = ((), (), s32[]{:S(2)}) async-start(), calls=%async_computation.31 | async-start | bytes 14155776 | tf_op jit(solution)/shard_map/all_gather | solution.py:107
  10.6 303.4 %all-gather.20.cloned.1.call-start = ((), (), s32[]{:S(2)}) async-start(), calls=%async_computation.32 | async-start | bytes 14155776 | tf_op jit(solution)/shard_map/all_gather | solution.py:108
  11.2 376.8 %all-gather.22.cloned.1.call-start = ((), (), s32[]{:S(2)}) async-start(), calls=%async_computation.33 | async-start | bytes 14155776 | tf_op jit(solution)/shard_map/all_gather | solution.py:109
  30.1 146.2 %copy-start.73 = (f32[1536]{0:T(1024)}, f32[1536]{0:T(1024)S(1)}, u32[]{:S(2)}) copy-start(f32[1536]{0:T(1024)S(1)} %convert_element_type.330) | copy-start | bytes 18436
  46.7 87.3 %copy-start.81 = (f32[128]{0:T(128)}, f32[128]{0:T(128)S(1)}, u32[]{:S(2)}) copy-start(f32[128]{0:T(128)S(1)} %get-tuple-element.737) | copy-start | bytes 1540
  46.7 129.5 %copy-start.77 = (f32[128]{0:T(128)}, f32[128]{0:T(128)S(1)}, u32[]{:S(2)}) copy-start(f32[128]{0:T(128)S(1)} %get-tuple-element.738) | copy-start | bytes 1540
  52.8 25.0 %all-to-all-start.4 = ((bf16[128,8,96]{0,2,1:T(8,128)(2,1)}), bf16[128,8,96]{0,2,1:T(8,128)(2,1)S(1)}, u32[]{:S(2)}, u32[]{:S(2)}) async-start(bf16[128,8,96]{0,2,1:T(8,128)(2,1)} %bitcast.29), calls=%async_computation.4 | async-start | bytes 393216 | tf_op jit(solution)/shard_map/all_to_all | solution.py:122
  77.8 12.6 all-to-all-start.6
  90.5 10.3 all-to-all-start
  100.8 37.3 %all-to-all-start.2 = ((bf16[128,8,96]{0,2,1:T(8,128)(2,1)}), bf16[128,8,96]{0,2,1:T(8,128)(2,1)S(1)}, u32[]{:S(2)}, u32[]{:S(2)}) async-start(bf16[128,8,96]{0,2,1:T(8,128)(2,1)} %bitcast.13), calls=%async_computation.2 | async-start | bytes 393216 | tf_op jit(solution)/shard_map/all_to_all | solution.py:123
  119.2 70.9 %copy-start.52 = (bf16[2048,2,96]{0,2,1:T(8,128)(2,1)}, bf16[2048,2,96]{0,2,1:T(8,128)(2,1)S(1)}, u32[]{:S(2)}) copy-start(bf16[2048,2,96]{0,2,1:T(8,128)(2,1)S(1)} %all_gather.73) | copy-start | bytes 2359300
  138.0 44.7 %all-to-all-start.5 = ((bf16[128,16,96]{0,2,1:T(8,128)(2,1)}), bf16[128,16,96]{0,2,1:T(8,128)(2,1)S(1)}, u32[]{:S(2)}, u32[]{:S(2)}) async-start(bf16[128,16,96]{0,2,1:T(8,128)(2,1)} %bitcast.34), calls=%async_computation.5 | async-start | bytes 786432 | tf_op jit(solution)/shard_map/all_to_all | solution.py:121
  182.8 22.0 %all-to-all-start.1 = ((bf16[128,16,96]{0,2,1:T(8,128)(2,1)}), bf16[128,16,96]{0,2,1:T(8,128)(2,1)}, u32[]{:S(2)}, u32[]{:S(2)}) async-start(bf16[128,16,96]{0,2,1:T(8,128)(2,1)} %bitcast.9), calls=%async_computation.1 | async-start | bytes 786432 | tf_op jit(solution)/shard_map/all_to_all | solution.py:121
  204.7 22.1 %all-to-all-start.7 = ((bf16[512,4,96]{2,1,0:T(4,128)(2,1)}), bf16[512,4,96]{2,1,0:T(4,128)(2,1)S(1)}, u32[]{:S(2)}, u32[]{:S(2)}) async-start(bf16[512,4,96]{2,1,0:T(4,128)(2,1)} %copy.188), calls=%async_computation.7 | async-start | bytes 1048576 | tf_op jit(solution)/shard_map/all_to_all | solution.py:175
  226.9 16.0 %all-to-all-start.3 = ((bf16[512,4,96]{2,1,0:T(4,128)(2,1)}), bf16[512,4,96]{2,1,0:T(4,128)(2,1)}, u32[]{:S(2)}, u32[]{:S(2)}) async-start(bf16[512,4,96]{2,1,0:T(4,128)(2,1)} %copy.178), calls=%async_computation.3 | async-start | bytes 1048576 | tf_op jit(solution)/shard_map/all_to_all | solution.py:175
  250.1 63.8 %copy-start.17 = (bf16[128,1536]{1,0:T(8,128)(2,1)}, bf16[128,1536]{1,0:T(8,128)(2,1)S(1)}, u32[]{:S(2)}) copy-start(bf16[128,1536]{1,0:T(8,128)(2,1)S(1)} %multiply_convert_fusion.7) | copy-start | bytes 1179652
  258.6 129.4 %copy-start.43 = (bf16[2,1,128,1536]{3,2,1,0:T(8,128)(2,1)S(1)}, bf16[2,1,128,1536]{3,2,1,0:T(8,128)(2,1)}, u32[]{:S(2)}) copy-start(bf16[2,1,128,1536]{3,2,1,0:T(8,128)(2,1)} %param.18) | copy-start | bytes 2359300
  464.9 16.7 %all-to-all-start.12 = ((bf16[128,16,96]{0,2,1:T(8,128)(2,1)}), bf16[128,16,96]{0,2,1:T(8,128)(2,1)S(1)}, u32[]{:S(2)}, u32[]{:S(2)}) async-start(bf16[128,16,96]{0,2,1:T(8,128)(2,1)} %bitcast.79), calls=%async_computation.14 | async-start | bytes 786432 | tf_op jit(solution)/shard_map/all_to_all | solution.py:203
  481.6 60.2 %all-to-all-start.8 = ((bf16[128,16,96]{0,2,1:T(8,128)(2,1)}), bf16[128,16,96]{0,2,1:T(8,128)(2,1)}, u32[]{:S(2)}, u32[]{:S(2)}) async-start(bf16[128,16,96]{0,2,1:T(8,128)(2,1)} %bitcast.57), calls=%async_computation.8 | async-start | bytes 786432 | tf_op jit(solution)/shard_map/all_to_all | solution.py:203
  485.7 111.4 %reduce-scatter.16.cloned.1.call-start = ((), (), s32[]{:S(2)}) async-start(), calls=%async_computation.36 | async-start | bytes 983040 | tf_op jit(solution)/shard_map/reduce_scatter | solution.py:269
  541.8 78.7 %reduce-scatter.12.cloned.1.call-start = ((), (), s32[]{:S(2)}) async-start(), calls=%async_computation.34 | async-start | bytes 983040 | tf_op jit(solution)/shard_map/reduce_scatter | solution.py:269
  593.8 56.1 %reduce-scatter.18.cloned.1.call-start = ((), (), s32[]{:S(2)}) async-start(), calls=%async_computation.37 | async-start | bytes 983040 | tf_op jit(solution)/shard_map/reduce_scatter | solution.py:272
  593.9 42.1 %copy-start.7 = (bf16[2,1,128,1536]{3,2,1,0:T(8,128)(2,1)S(1)}, bf16[2,1,128,1536]{3,2,1,0:T(8,128)(2,1)}, u32[]{:S(2)}) copy-start(bf16[2,1,128,1536]{3,2,1,0:T(8,128)(2,1)} %param.16) | copy-start | bytes 2359300
  593.9 42.1 %copy-start.74 = (f32[1536]{0:T(1024)S(1)}, f32[1536]{0:T(1024)}, u32[]{:S(2)}) copy-start(f32[1536]{0:T(1024)} %copy-done.73) | copy-start | bytes 18436
  593.9 42.1 %copy-start.78 = (f32[128]{0:T(128)S(1)}, f32[128]{0:T(128)}, u32[]{:S(2)}) copy-start(f32[128]{0:T(128)} %copy-done.77) | copy-start | bytes 1540
  596.1 82.8 %reduce-scatter.14.cloned.1.call-start = ((), (), s32[]{:S(2)}) async-start(), calls=%async_computation.35 | async-start | bytes 983040 | tf_op jit(solution)/shard_map/reduce_scatter | solution.py:272
  599.0 23.3 %all-to-all-start.14 = ((bf16[512,2,96]{2,1,0:T(2,128)(2,1)}), bf16[512,2,96]{2,1,0:T(2,128)(2,1)S(1)}, u32[]{:S(2)}, u32[]{:S(2)}) async-start(bf16[512,2,96]{2,1,0:T(2,128)(2,1)} %copy.208), calls=%async_computation.17 | async-start | bytes 524288 | tf_op jit(solution)/shard_map/all_to_all | solution.py:287
  622.3 13.5 all-to-all-start.10
  626.9 196.2 %reduce-scatter.22.cloned.1.call-start = ((), (), s32[]{:S(2)}) async-start(), calls=%async_computation.39 | async-start | bytes 2654208 | tf_op jit(solution)/shard_map/reduce_scatter | solution.py:334
  651.7 29.0 %all-to-all-start.15 = ((bf16[512,2,96]{2,1,0:T(2,128)(2,1)}), bf16[512,2,96]{2,1,0:T(2,128)(2,1)S(1)}, u32[]{:S(2)}, u32[]{:S(2)}) async-start(bf16[512,2,96]{2,1,0:T(2,128)(2,1)} %copy.212), calls=%async_computation.19 | async-start | bytes 524288 | tf_op jit(solution)/shard_map/all_to_all | solution.py:290
  680.7 13.5 all-to-all-start.11
  685.3 137.8 %reduce-scatter.24.cloned.1.call-start = ((), (), s32[]{:S(2)}) async-start(), calls=%async_computation.40 | async-start | bytes 2654208 | tf_op jit(solution)/shard_map/reduce_scatter | solution.py:334
  697.7 131.5 %reduce-scatter.26.cloned.1.call-start = ((), (), s32[]{:S(2)}) async-start(), calls=%async_computation.41 | async-start | bytes 5308416 | tf_op jit(solution)/shard_map/reduce_scatter | solution.py:334
  704.1 13.8 all-to-all-start.9
  717.9 13.3 all-to-all-start.13
  721.3 165.4 %reduce-scatter.20.cloned.1.call-start = ((), (), s32[]{:S(2)}) async-start(), calls=%async_computation.38 | async-start | bytes 5308416 | tf_op jit(solution)/shard_map/reduce_scatter | solution.py:334
  738.6 244.0 %reduce-scatter.28.cloned.1.call-start = ((), (), s32[]{:S(2)}) async-start(), calls=%async_computation.42 | async-start | bytes 14155776 | tf_op jit(solution)/shard_map/reduce_scatter | solution.py:334
  766.4 312.0 %reduce-scatter.30.cloned.1.call-start = ((), (), s32[]{:S(2)}) async-start(), calls=%async_computation.43 | async-start | bytes 14155776 | tf_op jit(solution)/shard_map/reduce_scatter | solution.py:334
  794.9 379.3 %reduce-scatter.32.cloned.1.call-start = ((), (), s32[]{:S(2)}) async-start(), calls=%async_computation.44 | async-start | bytes 14155776 | tf_op jit(solution)/shard_map/reduce_scatter | solution.py:334
  822.8 352.0 %copy-start.79 = (f32[1536]{0:T(1024)S(1)}, f32[1536]{0:T(1024)}, u32[]{:S(2)}) copy-start(f32[1536]{0:T(1024)} %get-tuple-element.608) | copy-start | bytes 18436
  822.8 352.0 %copy-start.80 = (f32[1536]{0:T(1024)S(1)}, f32[1536]{0:T(1024)}, u32[]{:S(2)}) copy-start(f32[1536]{0:T(1024)} %get-tuple-element.606) | copy-start | bytes 18436
  822.8 352.0 %copy-start.11 = (f32[128,1536]{1,0:T(8,128)S(1)}, f32[128,1536]{1,0:T(8,128)}, u32[]{:S(2)}) copy-start(f32[128,1536]{1,0:T(8,128)} %get-tuple-element.733) | copy-start | bytes 2359300
  822.8 585.8 %all-reduce.10.cloned.1.call-start = ((), (), s32[]{:S(2)}) async-start(), calls=%async_computation.45 | async-start | bytes 12976128 | tf_op jit(solution)/shard_map/psum | solution.py:336
  (123 other events, 777.6 us)
Sparse Core Ops, SparseCore 0:
  9.9 32.1 all-gather.9
  44.0 28.9 all-gather.13
  75.0 42.0 all-gather.11
  118.8 46.9 all-gather.15
  167.6 72.4 all-gather.17
  241.8 72.1 all-gather.19
  315.9 72.1 all-gather.21
  541.9 26.5 reduce-scatter.15
  593.9 26.4 reduce-scatter.11
  623.8 26.0 reduce-scatter.17
  652.8 26.0 reduce-scatter.13
  682.7 42.4 reduce-scatter.21
  729.5 42.4 reduce-scatter.23
  775.3 53.8 reduce-scatter.25
  832.9 53.8 reduce-scatter.19
  890.1 92.3 reduce-scatter.27
  985.9 92.3 reduce-scatter.29
  1081.7 92.3 reduce-scatter.31
  1177.1 231.4 all-reduce.9
